TPU v7x, 128 devices: a whole 4x4x4 slice. The times are simulated.
128 devices in a mesh: row: 8 (over z, core), col: 16 (over y, x).
Axes of the slice: x: 4, y: 4, z: 4, core: 2. Of those that a mesh axis runs over, the one named last changes fastest.
Arguments:
- kernel: float32 [16384, 16384], P('row', 'col'), may hold values from 0 to 3, as said below
Outputs:
- trailing: float32 [16384, 16384], P('row', 'col')
- factor_t: float32 [1024, 16384], P('col', 'row')
Inputs may be any that keep to these rules, and one draw needn't show every extreme that they name: K is symmetric: an RBF kernel over 256 donor features plus each donor's noise variance, of 0.5 or more, on the diagonal.
All inputs are finite; a program needn't handle non-finite values.
Results may differ from a plain program's by a relative error of at most 0.0003.
Values sent between devices are 32-bit elements; how exact they have to be, the bound alone decides.
A program may use at most 128 MiB of HBM per device.

v0:
```python
import jax
import jax.numpy as jnp
from jax import lax
from jax.sharding import PartitionSpec as P

PANEL = 512
PANELS = 2


def from_root(value, axis, source):
    kept = jnp.where(lax.axis_index(axis) == source, value, 0).astype(value.dtype)
    return lax.psum(kept, axis)


def outer_update(left_fac, right_fac):
    return lax.dot_general(
        left_fac,
        right_fac,
        (((0,), (0,)), ((), ())),
        precision=lax.Precision.HIGHEST,
        preferred_element_type=jnp.float32,
    )


def local(kernel):
    grid_rows = lax.axis_size("row")
    grid_cols = lax.axis_size("col")
    my_row = lax.axis_index("row")
    my_col = lax.axis_index("col")
    rows_loc = kernel.shape[0]
    cols_loc = kernel.shape[1]
    tile_w = PANEL // grid_cols
    spread = grid_cols // grid_rows
    row_local = jnp.arange(rows_loc, dtype=jnp.int32)
    row_ids = (row_local // tile_w * grid_rows + my_row) * tile_w + row_local % tile_w
    col_local = jnp.arange(cols_loc, dtype=jnp.int32)
    col_ids = (col_local // tile_w * grid_cols + my_col) * tile_w + col_local % tile_w
    down_list = []
    schur = kernel
    for panel_idx in range(PANELS):
        column_tile = schur[:, panel_idx * tile_w : (panel_idx + 1) * tile_w]
        first_col = panel_idx * PANEL
        first_tile = panel_idx * spread
        corner = column_tile[first_tile * tile_w : (first_tile + spread) * tile_w]
        flat_block = corner.reshape(1, spread * tile_w * tile_w)
        blocks = lax.all_gather(flat_block, ("row", "col"), axis=0, tiled=True)
        blocks = blocks.reshape(grid_rows, grid_cols, spread, tile_w, tile_w)
        blocks = blocks.transpose(2, 0, 3, 1, 4).reshape(PANEL, PANEL)
        lower_fac = jnp.linalg.cholesky(blocks)
        columns_t = column_tile.T
        gathered = lax.all_gather(columns_t, "col", axis=0, tiled=True)
        factor_loc = jax.scipy.linalg.solve_triangular(lower_fac, gathered, lower=True)
        factor_loc = jnp.where(row_ids[None, :] >= first_col, factor_loc, 0.0)
        picked = factor_loc.reshape(PANEL, cols_loc // tile_w, spread, tile_w)
        picked = lax.dynamic_index_in_dim(picked, my_col // grid_rows, 2, keepdims=False)
        picked = picked.reshape(PANEL, cols_loc)
        across = from_root(picked, "row", my_col % grid_rows)
        factor_loc, across = (factor_loc, across)
        schur = schur - outer_update(factor_loc, across)
        down_list.append(factor_loc)
    limit = PANELS * PANEL
    keep = (row_ids[:, None] >= limit) & (col_ids[None, :] >= limit)
    trailing = jnp.where(keep, schur, 0.0)
    stacked = jnp.concatenate(down_list, axis=0)
    per_col = PANELS * PANEL // grid_cols
    factor_out = lax.dynamic_slice_in_dim(stacked, my_col * per_col, per_col, 0)
    return (trailing, factor_out)


def solution(mesh):
    return jax.shard_map(
        local,
        mesh=mesh,
        in_specs=(P("row", "col"),),
        out_specs=(P("row", "col"), P("col", "row")),
        check_vma=False,
    )
```

profile of v0, /device:TPU:0, one launch (start us, length us, event | category | flops | bytes accessed | tf_op | source)
XLA Modules:
  0.0 662.9 jit_solution(6436545868017596230)
XLA Ops:
  8.7 9.1 %copy.22 = f32[2048,1024]{0,1:T(8,128)} copy(f32[2048,1024]{1,0:T(8,128)} %param.4) | data formatting | bytes 16777216 | tf_op args[0]
  19.7 57.2 %all-gather.11.cloned.1.call-done = f32[128,1,2048]{2,1,0:T(1,128)} async-done(((f32[1,1,2048]{2,1,0:T(1,128)}), f32[128,1,2048]{2,1,0:T(1,128)}) %all-gather.11.cloned.1.call-update) | async-done | bytes 1048592 | tf_op jit(solution)/shard_map/all_gather | solution.py:46
  76.8 3.7 reduce.16
  83.3 5.6 copy.18
  93.2 11.7 %cholesky.286 = f32[128,128]{1,0:T(8,128)S(1)} custom-call(f32[128,128]{1,0:T(8,128)S(1)} %cholesky.426), custom_call_target="Cholesky" | custom-call | tf_op jit(solution)/shard_map/jit(cholesky)/cholesky | solution.py:49
  105.0 9.8 %custom-call.27 = f32[1,128,128]{1,2,0:T(8,128)S(1)} custom-call(f32[1,128,128]{2,1,0:T(8,128)S(1)} %get-tuple-element.65), custom_call_target="InvertDiagBlocksLowerTriangular" | custom-call | tf_op jit(solution)/shard_map/jit(cholesky)/cholesky | solution.py:49
  115.6 11.7 %cholesky.305 = f32[128,128]{1,0:T(8,128)S(1)} custom-call(f32[128,128]{1,0:T(8,128)S(1)} %cholesky.430), custom_call_target="Cholesky" | custom-call | tf_op jit(solution)/shard_map/jit(cholesky)/cholesky | solution.py:49
  127.3 10.0 %custom-call.28 = f32[1,128,128]{1,2,0:T(8,128)S(1)} custom-call(f32[1,128,128]{2,1,0:T(8,128)S(1)} %get-tuple-element.62), custom_call_target="InvertDiagBlocksLowerTriangular" | custom-call | tf_op jit(solution)/shard_map/jit(cholesky)/cholesky | solution.py:49
  138.0 11.7 %cholesky.326 = f32[128,128]{1,0:T(8,128)S(1)} custom-call(f32[128,128]{1,0:T(8,128)S(1)} %cholesky.435), custom_call_target="Cholesky" | custom-call | tf_op jit(solution)/shard_map/jit(cholesky)/cholesky | solution.py:49
  149.7 9.8 %custom-call.29 = f32[1,128,128]{1,2,0:T(8,128)S(1)} custom-call(f32[1,128,128]{2,1,0:T(8,128)S(1)} %get-tuple-element.59), custom_call_target="InvertDiagBlocksLowerTriangular" | custom-call | tf_op jit(solution)/shard_map/jit(cholesky)/cholesky | solution.py:49
  160.2 11.7 %cholesky.343 = f32[128,128]{1,0:T(8,128)S(1)} custom-call(f32[128,128]{1,0:T(8,128)S(1)} %convolution_subtract_fusion.10), custom_call_target="Cholesky" | custom-call | tf_op jit(solution)/shard_map/jit(cholesky)/cholesky | solution.py:49
  176.5 8.2 %while.4 = (s32[]{:T(128)}, f32[512,512]{1,0:T(8,128)S(1)}, s32[4,2]{0,1:T(2,128)S(1)}, f32[4,128,128]{2,1,0:T(8,128)S(1)}, s32[]{:T(128)}) while((s32[]{:T(128)}, f32[512,512]{1,0:T(8,128)S(1)}, s32[4,2]{0,1:T(2,128)S(1)}, f32[4,128,128]{2,1,0:T(8,128)S(1)}, s32[]{:T(128)}) %tuple.58), condition=%wide.while_cond, body=%wide.while_body.sunk | while | flops 2 | bytes 131181 | solution.py:52
  184.8 39.3 %custom-call.30 = f32[4,128,128]{1,2,0:T(8,128)S(1)} custom-call(f32[4,128,128]{2,1,0:T(8,128)S(1)} %get-tuple-element.18), custom_call_target="InvertDiagBlocksLowerTriangular" | custom-call | tf_op jit(solution)/shard_map/jit(_solve_triangular)/triangular_solve | solution.py:52
  237.8 5.3 copy.21
  246.5 63.6 %all-reduce.4.cloned.1.call-done = f32[512,1024]{0,1:T(8,128)} async-done(((f32[512,1024]{0,1:T(8,128)}), f32[512,1024]{0,1:T(8,128)}) %all-reduce.4.cloned.1.call-update) | async-done | bytes 2097168 | tf_op jit(solution)/shard_map/psum | solution.py:12
  310.2 17.0 %convolution_subtract_fusion = f32[2048,1024]{0,1:T(8,128)S(1)} fusion(f32[2048,1024]{0,1:T(8,128)} %copy.22, f32[512,2048]{1,0:T(8,128)} %maximum_select_fusion, f32[512,1024]{0,1:T(8,128)} %all-reduce.4.cloned.1.call-done), kind=kOutput, calls=%fused_computation.9 | convolution fusion | flops 12886999040 | bytes 23068672 | tf_op jit(solution)/shard_map/dot_general | solution.py:16
  333.3 61.3 %all-gather.13.cloned.1.call-done = f32[128,1,2048]{2,1,0:T(1,128)} async-done(((f32[1,1,2048]{2,1,0:T(1,128)}), f32[128,1,2048]{2,1,0:T(1,128)}) %all-gather.13.cloned.1.call-update) | async-done | bytes 1048592 | tf_op jit(solution)/shard_map/all_gather | solution.py:46
  401.0 5.6 copy.24
  406.6 3.8 reshape.157
  411.0 11.7 %cholesky.358 = f32[128,128]{1,0:T(8,128)S(1)} custom-call(f32[128,128]{1,0:T(8,128)S(1)} %cholesky.439), custom_call_target="Cholesky" | custom-call | tf_op jit(solution)/shard_map/jit(cholesky)/cholesky | solution.py:49
  422.8 9.8 %custom-call.31 = f32[1,128,128]{1,2,0:T(8,128)S(1)} custom-call(f32[1,128,128]{2,1,0:T(8,128)S(1)} %get-tuple-element.55), custom_call_target="InvertDiagBlocksLowerTriangular" | custom-call | tf_op jit(solution)/shard_map/jit(cholesky)/cholesky | solution.py:49
  433.3 11.7 %cholesky.377 = f32[128,128]{1,0:T(8,128)S(1)} custom-call(f32[128,128]{1,0:T(8,128)S(1)} %cholesky.443), custom_call_target="Cholesky" | custom-call | tf_op jit(solution)/shard_map/jit(cholesky)/cholesky | solution.py:49
  445.1 10.2 %custom-call.32 = f32[1,128,128]{1,2,0:T(8,128)S(1)} custom-call(f32[1,128,128]{2,1,0:T(8,128)S(1)} %get-tuple-element.52), custom_call_target="InvertDiagBlocksLowerTriangular" | custom-call | tf_op jit(solution)/shard_map/jit(cholesky)/cholesky | solution.py:49
  455.9 11.7 %cholesky.398 = f32[128,128]{1,0:T(8,128)S(1)} custom-call(f32[128,128]{1,0:T(8,128)S(1)} %cholesky.448), custom_call_target="Cholesky" | custom-call | tf_op jit(solution)/shard_map/jit(cholesky)/cholesky | solution.py:49
  467.7 9.8 %custom-call.33 = f32[1,128,128]{1,2,0:T(8,128)S(1)} custom-call(f32[1,128,128]{2,1,0:T(8,128)S(1)} %get-tuple-element.49), custom_call_target="InvertDiagBlocksLowerTriangular" | custom-call | tf_op jit(solution)/shard_map/jit(cholesky)/cholesky | solution.py:49
  478.1 11.7 %cholesky.415 = f32[128,128]{1,0:T(8,128)S(1)} custom-call(f32[128,128]{1,0:T(8,128)S(1)} %convolution_subtract_fusion.9), custom_call_target="Cholesky" | custom-call | tf_op jit(solution)/shard_map/jit(cholesky)/cholesky | solution.py:49
  495.0 7.6 %while.5 = (s32[]{:T(128)}, f32[512,512]{1,0:T(8,128)S(1)}, s32[4,2]{0,1:T(2,128)S(1)}, f32[4,128,128]{2,1,0:T(8,128)S(1)}, s32[]{:T(128)}) while((s32[]{:T(128)}, f32[512,512]{1,0:T(8,128)S(1)}, s32[4,2]{0,1:T(2,128)S(1)}, f32[4,128,128]{2,1,0:T(8,128)S(1)}, s32[]{:T(128)}) %tuple.76), condition=%wide.while_cond.clone, body=%wide.while_body.clone.sunk | while | flops 2 | bytes 131181 | solution.py:52
  502.7 39.3 %custom-call.34 = f32[4,128,128]{1,2,0:T(8,128)S(1)} custom-call(f32[4,128,128]{2,1,0:T(8,128)S(1)} %get-tuple-element.19), custom_call_target="InvertDiagBlocksLowerTriangular" | custom-call | tf_op jit(solution)/shard_map/jit(_solve_triangular)/triangular_solve | solution.py:52
  555.7 5.3 copy.26
  566.3 61.8 %all-reduce.6.cloned.1.call-done = f32[512,1024]{0,1:T(8,128)} async-done(((f32[512,1024]{0,1:T(8,128)}), f32[512,1024]{0,1:T(8,128)}) %all-reduce.6.cloned.1.call-update) | async-done | bytes 2097168 | tf_op jit(solution)/shard_map/psum | solution.py:12
  628.2 18.4 %subtract_select_fusion = f32[2048,1024]{0,1:T(8,128)} fusion(f32[2048,1024]{0,1:T(8,128)} %copy-done, pred[2048]{0:T(1024)(128)(4,1)S(1)} %broadcast_compare_fusion.1, pred[1024]{0:T(1024)(128)(4,1)S(1)} %fusion.86, f32[512,2048]{1,0:T(8,128)} %maximum_select_fusion.1, f32[512,1024]{0,1:T(8,128)} %all-reduce.6.cloned.1.call-done), kind=kOutput, calls=%fused_computation.6 | convolution fusion | flops 12891193344 | bytes 23071744 | tf_op jit(solution)/shard_map/dot_general | solution.py:16
  646.5 9.2 %copy.28 = f32[2048,1024]{1,0:T(8,128)} copy(f32[2048,1024]{0,1:T(8,128)} %subtract_select_fusion) | data formatting | bytes 16777216
  (123 shorter events, 83.7 us)
Async XLA Ops:
  7.2 69.7 %all-gather.11.cloned.1.call-start = ((), (), s32[]{:S(2)}) async-start(), calls=%async_computation.4 | async-start | bytes 1056768 | tf_op jit(solution)/shard_map/all_gather | solution.py:46
  8.7 215.4 %all-gather.7.cloned.1.call-start = ((), (), s32[]{:S(2)}) async-start(), calls=%async_computation | async-start | bytes 4456448 | tf_op jit(solution)/shard_map/all_gather | solution.py:51
  19.6 290.6 %all-reduce.4.cloned.1.call-start = ((), (), s32[]{:S(2)}) async-start(), calls=%async_computation.1 | async-start | bytes 4194304 | tf_op jit(solution)/shard_map/psum | solution.py:12
  224.1 5.7 copy-start.1
  246.5 148.0 %all-gather.13.cloned.1.call-start = ((), (), s32[]{:S(2)}) async-start(), calls=%async_computation.5 | async-start | bytes 1056768 | tf_op jit(solution)/shard_map/all_gather | solution.py:46
  327.2 3.4 copy-start
  331.5 210.6 %all-gather.9.cloned.1.call-start = ((), (), s32[]{:S(2)}) async-start(), calls=%async_computation.2 | async-start | bytes 4456448 | tf_op jit(solution)/shard_map/all_gather | solution.py:51
  333.2 295.0 %all-reduce.6.cloned.1.call-start = ((), (), s32[]{:S(2)}) async-start(), calls=%async_computation.3 | async-start | bytes 4194304 | tf_op jit(solution)/shard_map/psum | solution.py:12
  542.0 5.7 copy-start.2
Sparse Core Ops, SparseCore 0:
  10.8 65.9 all-gather.10
  79.5 49.2 all-gather.6
  246.6 63.5 all-reduce.3
  331.6 62.9 all-gather.12
  397.1 49.4 all-gather.8
  564.5 63.6 all-reduce.5
where the time goes:
time: 668 us; the launch traced here: 663 us
  other arithmetic  258 us (39%)
  waiting for transfers between devices  244 us (37%)
  local copies, waits for them, and re-layouts  78.7 us (12%)
  matrix products  61.3 us (9%)
  between operations  19.7 us (3%)
    another operation x29, other arithmetic, local(): lower_fac = jnp.linalg.cholesky(blocks)  158 us
    psum x2, waiting for transfers between devices, from_root(): return lax.psum(kept, axis)  125 us
    all_gather x2, waiting for transfers between devices, local(): blocks = lax.all_gather(flat_block, ('row', 'col'), axis=0, tiled=True)  118 us
    another operation x5, other arithmetic, local(): jax.scipy.linalg.solve_triangular(lower_fac, gathered, lower=True)  78.9 us
    dot_general x2, matrix products, outer_update(): lax.dot_general(left_fac, right_fac, (((0,), (0,)), ((), ())), precision=...  35.4 us
    unnamed x10, local copies, waits for them, and re-layouts  23.1 us
    another operation x14, matrix products, local(): jax.scipy.linalg.solve_triangular(lower_fac, gathered, lower=True)  22.2 us
    another operation x27, local copies, waits for them, and re-layouts, local(): jax.scipy.linalg.solve_triangular(lower_fac, gathered, lower=True)  15.5 us
  transfers between devices with their start and end apart: 6, of which 4 were waited for; matrix products, arithmetic and copies ran while one was open for 46% of the time, Pallas kernels for 0%

commit v1 on v0

--- a/solution.py
+++ b/solution.py
@@ -43,7 +43,12 @@
         first_tile = panel_idx * spread
         corner = column_tile[first_tile * tile_w : (first_tile + spread) * tile_w]
         flat_block = corner.reshape(1, spread * tile_w * tile_w)
-        blocks = lax.all_gather(flat_block, ("row", "col"), axis=0, tiled=True)
+        blocks = jnp.concatenate(
+            lax.all_to_all(
+                jnp.stack([flat_block] * lax.axis_size(("row", "col"))), ("row", "col"), 0, 0
+            ),
+            axis=0,
+        )
         blocks = blocks.reshape(grid_rows, grid_cols, spread, tile_w, tile_w)
         blocks = blocks.transpose(2, 0, 3, 1, 4).reshape(PANEL, PANEL)
         lower_fac = jnp.linalg.cholesky(blocks)

time: 668 us -> 611 us (0.915)
  waiting for transfers between devices: 244 us -> 167 us
  starting transfers between devices: 0.25 us -> 19.3 us
    all_gather x2 -> x0, waiting for transfers between devices: 118 us -> none  [local(): blocks = lax.all_gather(flat_block, ('row', 'col'), axis=0, tiled=True)]
    all_to_all x0 -> x2, waiting for transfers between devices: none -> 45.7 us  [local(): lax.all_to_all(jnp.stack([flat_block] * lax.axis_size(('row', 'col'))), (...]
    all_to_all x0 -> x2, starting transfers between devices: none -> 19.2 us  [local(): lax.all_to_all(jnp.stack([flat_block] * lax.axis_size(('row', 'col'))), (...]
    another operation x0 -> x6, local copies, waits for them, and re-layouts: none -> 8.74 us  [the longest x2 5.45 us: local(): blocks = blocks.reshape(grid_rows, grid_cols, spread, tile_w, tile_w)]
    all_gather x2 -> x0, other arithmetic: 7.43 us -> none  [local(): blocks = lax.all_gather(flat_block, ('row', 'col'), axis=0, tiled=True)]
    unnamed x10 -> x8, local copies, waits for them, and re-layouts: 23.1 us -> 21.8 us
  transfers between devices with their start and end apart: 6 -> 6, of which waited for: 4 -> 4; matrix products, arithmetic and copies ran while one was open for 46% -> 49% of each run, Pallas kernels for 0% -> 0%
where the time goes in v1:
time: 611 us; the launch traced here: 604 us
  other arithmetic  256 us (42%)
  waiting for transfers between devices  167 us (27%)
  local copies, waits for them, and re-layouts  80.4 us (13%)
  matrix products  61.3 us (10%)
  between operations  19.4 us (3%)
  starting transfers between devices  19.3 us (3%)
    another operation x29, other arithmetic, local(): lower_fac = jnp.linalg.cholesky(blocks)  158 us
    psum x2, waiting for transfers between devices, from_root(): return lax.psum(kept, axis)  122 us
    another operation x5, other arithmetic, local(): jax.scipy.linalg.solve_triangular(lower_fac, gathered, lower=True)  78.9 us
    all_to_all x2, waiting for transfers between devices, local(): lax.all_to_all(jnp.stack([flat_block] * lax.axis_size(('row', 'col'))), (...  45.7 us
    dot_general x2, matrix products, outer_update(): lax.dot_general(left_fac, right_fac, (((0,), (0,)), ((), ())), precision=...  35.4 us
    another operation x14, matrix products, local(): jax.scipy.linalg.solve_triangular(lower_fac, gathered, lower=True)  22.2 us
    unnamed x8, local copies, waits for them, and re-layouts  21.8 us
    all_to_all x2, starting transfers between devices, local(): lax.all_to_all(jnp.stack([flat_block] * lax.axis_size(('row', 'col'))), (...  19.2 us
  transfers between devices with their start and end apart: 6, of which 4 were waited for; matrix products, arithmetic and copies ran while one was open for 49% of the time, Pallas kernels for 0%

profile of v1, /device:TPU:0, one launch (start us, length us, event | category | flops | bytes accessed | tf_op | source)
XLA Modules:
  0.0 604.3 jit_solution(7645060621133841516)
XLA Ops:
  7.2 9.1 %copy.22 = f32[2048,1024]{0,1:T(8,128)} copy(f32[2048,1024]{1,0:T(8,128)} %param.4) | data formatting | bytes 16777216 | tf_op args[0]
  20.4 11.1 %all-to-all-start = ((f32[128,1,2048]{2,1,0:T(1,128)}), f32[128,1,2048]{2,1,0:T(1,128)S(1)}, u32[]{:S(2)}, u32[]{:S(2)}) async-start(f32[128,1,2048]{2,1,0:T(1,128)} %stack.6), calls=%async_computation | async-start | bytes 2097152 | tf_op jit(solution)/shard_map/all_to_all | solution.py:47
  31.7 22.9 %all-to-all-done = f32[128,1,2048]{2,1,0:T(1,128)S(1)} async-done(((f32[128,1,2048]{2,1,0:T(1,128)}), f32[128,1,2048]{2,1,0:T(1,128)S(1)}, u32[]{:S(2)}, u32[]{:S(2)}) %all-to-all-start) | async-done | bytes 1048608 | tf_op jit(solution)/shard_map/all_to_all | solution.py:47
  59.8 5.6 copy.18
  69.7 11.7 %cholesky.286 = f32[128,128]{1,0:T(8,128)S(1)} custom-call(f32[128,128]{1,0:T(8,128)S(1)} %cholesky.426), custom_call_target="Cholesky" | custom-call | tf_op jit(solution)/shard_map/jit(cholesky)/cholesky | solution.py:54
  81.5 9.8 %custom-call.27 = f32[1,128,128]{1,2,0:T(8,128)S(1)} custom-call(f32[1,128,128]{2,1,0:T(8,128)S(1)} %get-tuple-element.65), custom_call_target="InvertDiagBlocksLowerTriangular" | custom-call | tf_op jit(solution)/shard_map/jit(cholesky)/cholesky | solution.py:54
  92.1 11.7 %cholesky.305 = f32[128,128]{1,0:T(8,128)S(1)} custom-call(f32[128,128]{1,0:T(8,128)S(1)} %cholesky.430), custom_call_target="Cholesky" | custom-call | tf_op jit(solution)/shard_map/jit(cholesky)/cholesky | solution.py:54
  103.8 10.0 %custom-call.28 = f32[1,128,128]{1,2,0:T(8,128)S(1)} custom-call(f32[1,128,128]{2,1,0:T(8,128)S(1)} %get-tuple-element.62), custom_call_target="InvertDiagBlocksLowerTriangular" | custom-call | tf_op jit(solution)/shard_map/jit(cholesky)/cholesky | solution.py:54
  114.5 11.7 %cholesky.326 = f32[128,128]{1,0:T(8,128)S(1)} custom-call(f32[128,128]{1,0:T(8,128)S(1)} %cholesky.435), custom_call_target="Cholesky" | custom-call | tf_op jit(solution)/shard_map/jit(cholesky)/cholesky | solution.py:54
  126.3 9.8 %custom-call.29 = f32[1,128,128]{1,2,0:T(8,128)S(1)} custom-call(f32[1,128,128]{2,1,0:T(8,128)S(1)} %get-tuple-element.59), custom_call_target="InvertDiagBlocksLowerTriangular" | custom-call | tf_op jit(solution)/shard_map/jit(cholesky)/cholesky | solution.py:54
  136.7 11.7 %cholesky.343 = f32[128,128]{1,0:T(8,128)S(1)} custom-call(f32[128,128]{1,0:T(8,128)S(1)} %convolution_subtract_fusion.10), custom_call_target="Cholesky" | custom-call | tf_op jit(solution)/shard_map/jit(cholesky)/cholesky | solution.py:54
  153.0 8.2 %while.4 = (s32[]{:T(128)}, f32[512,512]{1,0:T(8,128)S(1)}, s32[4,2]{0,1:T(2,128)S(1)}, f32[4,128,128]{2,1,0:T(8,128)S(1)}, s32[]{:T(128)}) while((s32[]{:T(128)}, f32[512,512]{1,0:T(8,128)S(1)}, s32[4,2]{0,1:T(2,128)S(1)}, f32[4,128,128]{2,1,0:T(8,128)S(1)}, s32[]{:T(128)}) %tuple.58), condition=%wide.while_cond, body=%wide.while_body.sunk | while | flops 2 | bytes 131181 | solution.py:57
  161.3 39.3 %custom-call.30 = f32[4,128,128]{1,2,0:T(8,128)S(1)} custom-call(f32[4,128,128]{2,1,0:T(8,128)S(1)} %get-tuple-element.18), custom_call_target="InvertDiagBlocksLowerTriangular" | custom-call | tf_op jit(solution)/shard_map/jit(_solve_triangular)/triangular_solve | solution.py:57
  214.3 5.3 copy.21
  223.1 61.8 %all-reduce.4.cloned.1.call-done = f32[512,1024]{0,1:T(8,128)} async-done(((f32[512,1024]{0,1:T(8,128)}), f32[512,1024]{0,1:T(8,128)}) %all-reduce.4.cloned.1.call-update) | async-done | bytes 2097168 | tf_op jit(solution)/shard_map/psum | solution.py:12
  284.9 17.0 %convolution_subtract_fusion = f32[2048,1024]{0,1:T(8,128)S(1)} fusion(f32[2048,1024]{0,1:T(8,128)} %copy.22, f32[512,2048]{1,0:T(8,128)} %maximum_select_fusion, f32[512,1024]{0,1:T(8,128)} %all-reduce.4.cloned.1.call-done), kind=kOutput, calls=%fused_computation.9 | convolution fusion | flops 12886999040 | bytes 23068672 | tf_op jit(solution)/shard_map/dot_general | solution.py:16
  308.6 8.0 %all-to-all-start.1 = ((f32[128,1,2048]{2,1,0:T(1,128)}), f32[128,1,2048]{2,1,0:T(1,128)S(1)}, u32[]{:S(2)}, u32[]{:S(2)}) async-start(f32[128,1,2048]{2,1,0:T(1,128)} %stack.7), calls=%async_computation.1 | async-start | bytes 2097152 | tf_op jit(solution)/shard_map/all_to_all | solution.py:47
  316.7 22.8 %all-to-all-done.1 = f32[128,1,2048]{2,1,0:T(1,128)S(1)} async-done(((f32[128,1,2048]{2,1,0:T(1,128)}), f32[128,1,2048]{2,1,0:T(1,128)S(1)}, u32[]{:S(2)}, u32[]{:S(2)}) %all-to-all-start.1) | async-done | bytes 1048608 | tf_op jit(solution)/shard_map/all_to_all | solution.py:47
  344.8 5.6 copy.24
  354.8 11.7 %cholesky.358 = f32[128,128]{1,0:T(8,128)S(1)} custom-call(f32[128,128]{1,0:T(8,128)S(1)} %cholesky.439), custom_call_target="Cholesky" | custom-call | tf_op jit(solution)/shard_map/jit(cholesky)/cholesky | solution.py:54
  366.6 9.8 %custom-call.31 = f32[1,128,128]{1,2,0:T(8,128)S(1)} custom-call(f32[1,128,128]{2,1,0:T(8,128)S(1)} %get-tuple-element.55), custom_call_target="InvertDiagBlocksLowerTriangular" | custom-call | tf_op jit(solution)/shard_map/jit(cholesky)/cholesky | solution.py:54
  377.1 11.7 %cholesky.377 = f32[128,128]{1,0:T(8,128)S(1)} custom-call(f32[128,128]{1,0:T(8,128)S(1)} %cholesky.443), custom_call_target="Cholesky" | custom-call | tf_op jit(solution)/shard_map/jit(cholesky)/cholesky | solution.py:54
  388.9 10.2 %custom-call.32 = f32[1,128,128]{1,2,0:T(8,128)S(1)} custom-call(f32[1,128,128]{2,1,0:T(8,128)S(1)} %get-tuple-element.52), custom_call_target="InvertDiagBlocksLowerTriangular" | custom-call | tf_op jit(solution)/shard_map/jit(cholesky)/cholesky | solution.py:54
  399.7 11.7 %cholesky.398 = f32[128,128]{1,0:T(8,128)S(1)} custom-call(f32[128,128]{1,0:T(8,128)S(1)} %cholesky.448), custom_call_target="Cholesky" | custom-call | tf_op jit(solution)/shard_map/jit(cholesky)/cholesky | solution.py:54
  411.5 9.8 %custom-call.33 = f32[1,128,128]{1,2,0:T(8,128)S(1)} custom-call(f32[1,128,128]{2,1,0:T(8,128)S(1)} %get-tuple-element.49), custom_call_target="InvertDiagBlocksLowerTriangular" | custom-call | tf_op jit(solution)/shard_map/jit(cholesky)/cholesky | solution.py:54
  421.9 11.7 %cholesky.415 = f32[128,128]{1,0:T(8,128)S(1)} custom-call(f32[128,128]{1,0:T(8,128)S(1)} %convolution_subtract_fusion.9), custom_call_target="Cholesky" | custom-call | tf_op jit(solution)/shard_map/jit(cholesky)/cholesky | solution.py:54
  438.8 7.6 %while.5 = (s32[]{:T(128)}, f32[512,512]{1,0:T(8,128)S(1)}, s32[4,2]{0,1:T(2,128)S(1)}, f32[4,128,128]{2,1,0:T(8,128)S(1)}, s32[]{:T(128)}) while((s32[]{:T(128)}, f32[512,512]{1,0:T(8,128)S(1)}, s32[4,2]{0,1:T(2,128)S(1)}, f32[4,128,128]{2,1,0:T(8,128)S(1)}, s32[]{:T(128)}) %tuple.72), condition=%wide.while_cond.clone, body=%wide.while_body.clone.sunk | while | flops 2 | bytes 131181 | solution.py:57
  446.5 39.3 %custom-call.34 = f32[4,128,128]{1,2,0:T(8,128)S(1)} custom-call(f32[4,128,128]{2,1,0:T(8,128)S(1)} %get-tuple-element.19), custom_call_target="InvertDiagBlocksLowerTriangular" | custom-call | tf_op jit(solution)/shard_map/jit(_solve_triangular)/triangular_solve | solution.py:57
  499.5 5.3 copy.26
  510.1 59.8 %all-reduce.6.cloned.1.call-done = f32[512,1024]{0,1:T(8,128)} async-done(((f32[512,1024]{0,1:T(8,128)}), f32[512,1024]{0,1:T(8,128)}) %all-reduce.6.cloned.1.call-update) | async-done | bytes 2097168 | tf_op jit(solution)/shard_map/psum | solution.py:12
  569.9 18.4 %subtract_select_fusion = f32[2048,1024]{0,1:T(8,128)} fusion(f32[2048,1024]{0,1:T(8,128)} %copy-done, pred[2048]{0:T(1024)(128)(4,1)S(1)} %broadcast_compare_fusion.1, pred[1024]{0:T(1024)(128)(4,1)S(1)} %fusion.86, f32[512,2048]{1,0:T(8,128)} %maximum_select_fusion.1, f32[512,1024]{0,1:T(8,128)} %all-reduce.6.cloned.1.call-done), kind=kOutput, calls=%fused_computation.6 | convolution fusion | flops 12891193344 | bytes 23071744 | tf_op jit(solution)/shard_map/dot_general | solution.py:16
  588.3 9.2 %copy.28 = f32[2048,1024]{1,0:T(8,128)} copy(f32[2048,1024]{0,1:T(8,128)} %subtract_select_fusion) | data formatting | bytes 16777216
  (123 shorter events, 90.4 us)
Async XLA Ops:
  7.2 193.5 %all-gather.3.cloned.1.call-start = ((), (), s32[]{:S(2)}) async-start(), calls=%async_computation.2 | async-start | bytes 4456448 | tf_op jit(solution)/shard_map/all_gather | solution.py:56
  20.4 34.1 %all-to-all-start = ((f32[128,1,2048]{2,1,0:T(1,128)}), f32[128,1,2048]{2,1,0:T(1,128)S(1)}, u32[]{:S(2)}, u32[]{:S(2)}) async-start(f32[128,1,2048]{2,1,0:T(1,128)} %stack.6), calls=%async_computation | async-start | bytes 2097152 | tf_op jit(solution)/shard_map/all_to_all | solution.py:47
  31.5 253.4 %all-reduce.4.cloned.1.call-start = ((), (), s32[]{:S(2)}) async-start(), calls=%async_computation.3 | async-start | bytes 4194304 | tf_op jit(solution)/shard_map/psum | solution.py:12
  200.6 5.7 copy-start.1
  223.0 262.8 %all-gather.5.cloned.1.call-start = ((), (), s32[]{:S(2)}) async-start(), calls=%async_computation.4 | async-start | bytes 4456448 | tf_op jit(solution)/shard_map/all_gather | solution.py:56
  301.9 3.4 copy-start
  308.6 30.9 %all-to-all-start.1 = ((f32[128,1,2048]{2,1,0:T(1,128)}), f32[128,1,2048]{2,1,0:T(1,128)S(1)}, u32[]{:S(2)}, u32[]{:S(2)}) async-start(f32[128,1,2048]{2,1,0:T(1,128)} %stack.7), calls=%async_computation.1 | async-start | bytes 2097152 | tf_op jit(solution)/shard_map/all_to_all | solution.py:47
  316.7 253.3 %all-reduce.6.cloned.1.call-start = ((), (), s32[]{:S(2)}) async-start(), calls=%async_computation.5 | async-start | bytes 4194304 | tf_op jit(solution)/shard_map/psum | solution.py:12
  485.8 5.7 copy-start.2
Sparse Core Ops, SparseCore 0:
  18.2 60.3 all-gather.2
  223.1 61.7 all-reduce.3
  306.2 57.4 all-gather.4
  508.3 61.5 all-reduce.5
